TPU v7x, 512 devices: a whole 4x8x8 slice. The times are simulated.
512 devices in a mesh: seq: 64 (over y, z), tp: 8 (over x, core).
Axes of the slice: x: 4, y: 8, z: 8, core: 2. Of those that a mesh axis runs over, the one named last changes fastest.
Arguments:
- queries: bfloat16 [16384, 4096], P('seq', 'tp'), may hold values from -6 to 6
- keys: bfloat16 [16384, 4096], P('seq', 'tp'), may hold values from -6 to 6
- values: bfloat16 [16384, 4096], P('seq', 'tp'), may hold values from -6 to 6
- out_cotangent: bfloat16 [16384, 2048], P('seq', 'tp'), may hold values from -16 to 16
- proj_weight: bfloat16 [4096, 2048], P('tp', 'seq'), may hold values from -0.125 to 0.125
Outputs:
- grad_queries: bfloat16 [16384, 4096], P('seq', 'tp')
- grad_keys: bfloat16 [16384, 4096], P('seq', 'tp')
- grad_values: bfloat16 [16384, 4096], P('seq', 'tp')
- grad_proj: float32 [4096, 2048], P('tp', 'seq')
All inputs are finite; a program needn't handle non-finite values.
Results may differ from a plain program's by a relative error of at most 0.0058.
Values may be sent and summed in bfloat16 or wider, within the bound.
No kernel may reach another device: no remote copies, remote signals or barrier semaphores. Data moves between devices by JAX's collectives and lax.ppermute only.
A program may use at most 128 MiB of HBM per device.

v0:
```python
import jax
import jax.numpy as jnp
from jax import lax
from jax.sharding import PartitionSpec as P

DH = 128


def entering(part, axis, combine, identity, reverse):
    count = lax.axis_size(axis)
    place = lax.axis_index(axis)
    ahead = count - 1 - place if reverse else place
    gathered = lax.all_gather(part, axis)
    state = jnp.zeros_like(part) + jnp.asarray(identity, part.dtype)

    def one(step, state):
        source = count - 1 - step if reverse else step
        return combine(state, lax.dynamic_index_in_dim(gathered, source, 0, False))

    return lax.fori_loop(0, ahead, one, state)


def add_pair(earlier, later_one):
    return earlier + later_one


def per_device(queries, keys, values, out_cotangent, proj_weight):
    tok = queries.shape[0]
    heads = queries.shape[1] // DH
    seq_count = lax.axis_size("seq")
    scale = 1.0 / jnp.sqrt(jnp.float32(DH * tok * seq_count))
    q_heads = queries.reshape(tok, heads, DH)
    k_heads = keys.reshape(tok, heads, DH)
    v_heads = values.reshape(tok, heads, DH)
    kv_state = jnp.einsum("thd,the->hde", k_heads, v_heads, preferred_element_type=jnp.float32)
    zero_state = jnp.zeros_like(kv_state)
    prior_sum = entering(kv_state, "seq", add_pair, zero_state, False)
    full_cot = lax.all_gather(out_cotangent, "tp", axis=1, tiled=True)
    grad_out = lax.dot_general(
        full_cot,
        lax.all_gather(proj_weight, "seq", axis=1, tiled=True),
        (((1,), (1,)), ((), ())),
        preferred_element_type=jnp.float32,
    ).astype(jnp.bfloat16)
    g_heads = grad_out.reshape(tok, heads, DH)
    qg_state = jnp.einsum("thd,the->hde", q_heads, g_heads, preferred_element_type=jnp.float32)
    later_sum = entering(qg_state, "seq", add_pair, zero_state, True)
    prior = prior_sum.astype(jnp.bfloat16)
    later = later_sum.astype(jnp.bfloat16)
    rows = jnp.arange(tok)
    causal = (rows[:, None] >= rows[None, :])[None]
    attn = jnp.where(
        causal,
        jnp.einsum("thd,shd->hts", q_heads, k_heads, preferred_element_type=jnp.float32),
        0.0,
    ).astype(jnp.bfloat16)
    back = jnp.where(
        causal,
        jnp.einsum("thd,shd->hts", g_heads, v_heads, preferred_element_type=jnp.float32),
        0.0,
    ).astype(jnp.bfloat16)
    attn_out = scale * (
        jnp.einsum("hts,she->the", attn, v_heads, preferred_element_type=jnp.float32)
        + jnp.einsum("thd,hde->the", q_heads, prior, preferred_element_type=jnp.float32)
    )
    grad_q = scale * (
        jnp.einsum("hts,shd->thd", back, k_heads, preferred_element_type=jnp.float32)
        + jnp.einsum("the,hde->thd", g_heads, prior, preferred_element_type=jnp.float32)
    )
    grad_k = scale * (
        jnp.einsum("hts,thd->shd", back, q_heads, preferred_element_type=jnp.float32)
        + jnp.einsum("she,hde->shd", v_heads, later, preferred_element_type=jnp.float32)
    )
    grad_v = scale * (
        jnp.einsum("hts,the->she", attn, g_heads, preferred_element_type=jnp.float32)
        + jnp.einsum("shd,hde->she", k_heads, later, preferred_element_type=jnp.float32)
    )
    out_flat = attn_out.astype(jnp.bfloat16).reshape(tok, heads * DH)
    proj_term = lax.dot_general(
        out_flat, full_cot, (((0,), (0,)), ((), ())), preferred_element_type=jnp.float32
    )
    proj_sum = lax.psum_scatter(proj_term, "seq", scatter_dimension=1, tiled=True)
    grad_proj = proj_sum / jnp.sqrt(jnp.float32(tok * seq_count))
    width = heads * DH
    return (
        grad_q.astype(jnp.bfloat16).reshape(tok, width),
        grad_k.astype(jnp.bfloat16).reshape(tok, width),
        grad_v.astype(jnp.bfloat16).reshape(tok, width),
        grad_proj,
    )


def solution(mesh):
    return jax.shard_map(
        per_device,
        mesh=mesh,
        in_specs=(P("seq", "tp"), P("seq", "tp"), P("seq", "tp"), P("seq", "tp"), P("tp", "seq")),
        out_specs=(P("seq", "tp"), P("seq", "tp"), P("seq", "tp"), P("tp", "seq")),
        check_vma=False,
    )
```

profile of v0, /device:TPU:2, one launch (start us, length us, event | category | flops | bytes accessed | tf_op | source)
XLA Modules:
  0.0 670.4 jit_solution(11894771848935743379)
XLA Ops:
  8.7 1.1 copy.56
  9.8 1.9 fusion.17
  11.8 31.1 %all-gather.7.cloned.1.call-done = bf16[256,2048]{1,0:T(8,128)(2,1)} async-done(((bf16[256,256]{1,0:T(8,128)(2,1)}), bf16[256,2048]{1,0:T(8,128)(2,1)}) %all-gather.7.cloned.1.call-update) | async-done | bytes 1048592 | tf_op jit(solution)/shard_map/all_gather | solution.py:38
  42.9 88.4 %all-gather.9.cloned.1.call-done = bf16[512,2048]{0,1:T(8,128)(2,1)} async-done(((bf16[512,32]{0,1:T(8,128)(2,1)}), bf16[512,2048]{0,1:T(8,128)(2,1)}) %all-gather.9.cloned.1.call-update) | async-done | bytes 2097168 | tf_op jit(solution)/shard_map/all_gather | solution.py:41
  131.3 2.6 convolution_convert_fusion
  135.9 135.8 %all-gather.11.cloned.1.call-done = f32[256,128,128]{2,1,0:T(8,128)} async-done(((f32[4,128,128]{2,1,0:T(8,128)}), f32[256,128,128]{2,1,0:T(8,128)}) %all-gather.11.cloned.1.call-update) | async-done | bytes 16777232 | tf_op jit(solution)/shard_map/all_gather | solution.py:13
  272.1 2.7 fusion.35
  277.1 136.3 %all-gather.13.cloned.1.call-done = f32[256,128,128]{2,1,0:T(8,128)} async-done(((f32[4,128,128]{2,1,0:T(8,128)}), f32[256,128,128]{2,1,0:T(8,128)}) %all-gather.13.cloned.1.call-update) | async-done | bytes 16777232 | tf_op jit(solution)/shard_map/all_gather | solution.py:13
  413.4 65.1 %while.23 = (s32[]{:T(128)}, f32[4,128,128]{2,1,0:T(8,128)S(1)}, s32[]{:T(128)}, f32[64,4,128,128]{3,2,1,0:T(8,128)}, s32[]{:T(128)}, /*index=5*/s32[]{:T(128)}, s32[]{:T(128)}, s32[]{:T(128)}) while((s32[]{:T(128)}, f32[4,128,128]{2,1,0:T(8,128)S(1)}, s32[]{:T(128)}, f32[64,4,128,128]{3,2,1,0:T(8,128)}, s32[]{:T(128)}, /*index=5*/s32[]{:T(128)}, ...), condition=%wide.region_3.4_spmd, body=%wide.region_2.3_spmd.sunk | while | flops 65542 | bytes 786575 | solution.py:20
  413.4 1.0 bitcast_add_fusion.5
  414.4 1.0 bitcast_add_fusion.5
  415.5 1.0 bitcast_add_fusion.5
  416.5 1.0 bitcast_add_fusion.5
  417.5 1.0 bitcast_add_fusion.5
  418.6 1.0 bitcast_add_fusion.5
  419.6 1.0 bitcast_add_fusion.5
  420.6 1.0 bitcast_add_fusion.5
  421.7 1.0 bitcast_add_fusion.5
  422.7 1.0 bitcast_add_fusion.5
  423.7 1.0 bitcast_add_fusion.5
  424.8 1.0 bitcast_add_fusion.5
  425.8 1.0 bitcast_add_fusion.5
  426.8 1.0 bitcast_add_fusion.5
  427.9 1.0 bitcast_add_fusion.5
  428.9 1.0 bitcast_add_fusion.5
  429.9 1.0 bitcast_add_fusion.5
  431.0 1.0 bitcast_add_fusion.5
  435.1 1.0 bitcast_add_fusion.5
  436.1 1.0 bitcast_add_fusion.5
  437.2 1.0 bitcast_add_fusion.5
  438.2 1.0 bitcast_add_fusion.5
  439.2 1.0 bitcast_add_fusion.5
  440.3 1.0 bitcast_add_fusion.5
  441.3 1.0 bitcast_add_fusion.5
  443.4 1.0 bitcast_add_fusion.5
  444.4 1.0 bitcast_add_fusion.5
  446.5 1.0 bitcast_add_fusion.5
  447.5 1.0 bitcast_add_fusion.5
  448.5 1.0 bitcast_add_fusion.5
  449.6 1.0 bitcast_add_fusion.5
  450.6 1.0 bitcast_add_fusion.5
  452.7 1.0 bitcast_add_fusion.5
  453.7 1.0 bitcast_add_fusion.5
  454.8 1.0 bitcast_add_fusion.5
  456.8 1.0 bitcast_add_fusion.5
  457.9 1.0 bitcast_add_fusion.5
  459.9 1.0 bitcast_add_fusion.5
  461.0 1.0 bitcast_add_fusion.5
  462.0 1.0 bitcast_add_fusion.5
  463.0 1.0 bitcast_add_fusion.5
  464.1 1.0 bitcast_add_fusion.5
  465.1 1.0 bitcast_add_fusion.5
  467.2 1.0 bitcast_add_fusion.5
  468.2 1.0 bitcast_add_fusion.5
  469.2 1.0 bitcast_add_fusion.5
  470.3 1.0 bitcast_add_fusion.5
  471.3 1.0 bitcast_add_fusion.5
  472.3 1.0 bitcast_add_fusion.5
  473.4 1.0 bitcast_add_fusion.5
  474.4 1.0 bitcast_add_fusion.5
  476.5 1.0 bitcast_add_fusion.5
  477.5 1.0 bitcast_add_fusion.5
  480.7 181.7 %reduce-scatter.2.cloned.1.call-done = f32[512,32]{0,1:T(8,128)} async-done(((f32[512,2048]{0,1:T(8,128)}), f32[512,32]{0,1:T(8,128)}) %reduce-scatter.2.cloned.1.call-update) | async-done | bytes 65552 | tf_op jit(solution)/shard_map/reduce_scatter | solution.py:82
  662.4 1.5 broadcast_multiply_fusion
  (46 shorter events, 18.3 us)
Async XLA Ops:
  7.2 126.9 %copy-start = (bf16[256,512]{1,0:T(8,128)(2,1)S(1)}, bf16[256,512]{1,0:T(8,128)(2,1)}, u32[]{:S(2)}) copy-start(bf16[256,512]{1,0:T(8,128)(2,1)} %param.9) | copy-start | bytes 786436
  7.2 128.1 %copy-start.1 = (bf16[256,512]{1,0:T(8,128)(2,1)S(1)}, bf16[256,512]{1,0:T(8,128)(2,1)}, u32[]{:S(2)}) copy-start(bf16[256,512]{1,0:T(8,128)(2,1)} %param.10) | copy-start | bytes 786436
  7.2 35.7 %all-gather.7.cloned.1.call-start = ((), (), s32[]{:S(2)}) async-start(), calls=%async_computation.1 | async-start | bytes 1179648 | tf_op jit(solution)/shard_map/all_gather | solution.py:38
  7.9 123.4 %all-gather.9.cloned.1.call-start = ((), (), s32[]{:S(2)}) async-start(), calls=%async_computation.2 | async-start | bytes 2129920 | tf_op jit(solution)/shard_map/all_gather | solution.py:41
  8.7 263.1 %all-gather.11.cloned.1.call-start = ((), (), s32[]{:S(2)}) async-start(), calls=%async_computation.4 | async-start | bytes 17039360 | tf_op jit(solution)/shard_map/all_gather | solution.py:13
  11.8 401.6 %all-gather.13.cloned.1.call-start = ((), (), s32[]{:S(2)}) async-start(), calls=%async_computation.5 | async-start | bytes 17039360 | tf_op jit(solution)/shard_map/all_gather | solution.py:13
  135.2 527.2 %reduce-scatter.2.cloned.1.call-start = ((), (), s32[]{:S(2)}) async-start(), calls=%async_computation.3 | async-start | bytes 4259840 | tf_op jit(solution)/shard_map/reduce_scatter | solution.py:82
  135.3 136.8 %copy-start.2 = (bf16[256,2048]{1,0:T(8,128)(2,1)S(1)}, bf16[256,2048]{1,0:T(8,128)(2,1)}, u32[]{:S(2)}) copy-start(bf16[256,2048]{1,0:T(8,128)(2,1)} %all-gather.7.cloned.1.call-done) | copy-start | bytes 3145732
Sparse Core Ops, SparseCore 0:
  10.1 32.7 all-gather.6
  45.9 85.3 all-gather.8
  134.9 136.7 all-gather.10
  275.2 138.1 all-gather.12
  417.3 245.0 reduce-scatter.1
where the time goes:
time: 673 us; the launch traced here: 670 us
  waiting for transfers between devices  575 us (85%)
  other arithmetic  65.2 us (10%)
  between operations  13.9 us (2%)
  matrix products  10.2 us (2%)
    all_gather x2, waiting for transfers between devices, entering(): gathered = lax.all_gather(part, axis)  272 us
    reduce_scatter x1, waiting for transfers between devices, per_device(): lax.psum_scatter(proj_term, 'seq', scatter_dimension=1, tiled=True)  182 us
    all_gather x1, waiting for transfers between devices, per_device(): lax.all_gather(proj_weight, 'seq', axis=1, tiled=True)  88.4 us
    add x63, other arithmetic, add_pair(): return earlier + later_one  63.7 us
    all_gather x1, waiting for transfers between devices, per_device(): full_cot = lax.all_gather(out_cotangent, 'tp', axis=1, tiled=True)  31.1 us
  transfers between devices with their start and end apart: 5, of which 5 were waited for; matrix products, arithmetic and copies ran while one was open for 12% of the time, Pallas kernels for 0%

commit v1 on v0

--- a/solution.py
+++ b/solution.py
@@ -35,7 +35,12 @@
     kv_state = jnp.einsum("thd,the->hde", k_heads, v_heads, preferred_element_type=jnp.float32)
     zero_state = jnp.zeros_like(kv_state)
     prior_sum = entering(kv_state, "seq", add_pair, zero_state, False)
-    full_cot = lax.all_gather(out_cotangent, "tp", axis=1, tiled=True)
+    ring = [out_cotangent]
+    for hop in range(7):
+        ring.append(lax.ppermute(ring[-1], "tp", [(dev, (dev + 1) % 8) for dev in range(8)]))
+    full_cot = jnp.roll(
+        jnp.concatenate(ring[::-1], axis=1), (lax.axis_index("tp") + 1) * ring[0].shape[1], axis=1
+    )
     grad_out = lax.dot_general(
         full_cot,
         lax.all_gather(proj_weight, "seq", axis=1, tiled=True),

time: 673 us -> 641 us (0.952)
  the two profiles are of different devices: /device:TPU:2 before, /device:TPU:4 now
where the time goes in v1:
time: 641 us; the launch traced here: 639 us
  waiting for transfers between devices  536 us (84%)
  other arithmetic  65.2 us (10%)
  between operations  14.1 us (2%)
  matrix products  11.1 us (2%)
  local copies, waits for them, and re-layouts  6.63 us (1%)
    all_gather x2, waiting for transfers between devices, entering(): gathered = lax.all_gather(part, axis)  271 us
    reduce_scatter x1, waiting for transfers between devices, per_device(): lax.psum_scatter(proj_term, 'seq', scatter_dimension=1, tiled=True)  182 us
    add x63, other arithmetic, add_pair(): return earlier + later_one  63.7 us
    all_gather x1, waiting for transfers between devices, per_device(): lax.all_gather(proj_weight, 'seq', axis=1, tiled=True)  55.1 us
    ppermute x7, waiting for transfers between devices, per_device(): lax.ppermute(ring[-1], 'tp', [(dev, (dev + 1) % 8) for dev in range(8)])  26.8 us
  transfers between devices with their start and end apart: 11, of which 11 were waited for; matrix products, arithmetic and copies ran while one was open for 13% of the time, Pallas kernels for 0%

profile of v1, /device:TPU:4, one launch (start us, length us, event | category | flops | bytes accessed | tf_op | source)
XLA Modules:
  0.0 638.8 jit_solution(16174519634430709755)
XLA Ops:
  8.0 1.1 copy.56
  9.1 1.9 fusion.20
  11.1 4.6 collective-permute-done
  15.7 4.4 collective-permute-done.1
  20.1 4.4 collective-permute-done.2
  24.5 4.4 collective-permute-done.3
  29.1 4.2 collective-permute-done.4
  33.3 1.4 collective-permute-start.5
  34.7 3.0 collective-permute-done.5
  37.7 2.6 collective-permute-start.6
  40.3 1.9 collective-permute-done.6
  44.3 55.1 %all-gather.6.cloned.1.call-done = bf16[512,2048]{0,1:T(8,128)(2,1)} async-done(((bf16[512,32]{0,1:T(8,128)(2,1)}), bf16[512,2048]{0,1:T(8,128)(2,1)}) %all-gather.6.cloned.1.call-update) | async-done | bytes 2097168 | tf_op jit(solution)/shard_map/all_gather | solution.py:46
  99.4 2.3 convolution_convert_fusion
  103.7 136.1 %all-gather.8.cloned.1.call-done = f32[256,128,128]{2,1,0:T(8,128)} async-done(((f32[4,128,128]{2,1,0:T(8,128)}), f32[256,128,128]{2,1,0:T(8,128)}) %all-gather.8.cloned.1.call-update) | async-done | bytes 16777232 | tf_op jit(solution)/shard_map/all_gather | solution.py:13
  240.1 3.9 fusion.13
  246.4 135.2 %all-gather.10.cloned.1.call-done = f32[256,128,128]{2,1,0:T(8,128)} async-done(((f32[4,128,128]{2,1,0:T(8,128)}), f32[256,128,128]{2,1,0:T(8,128)}) %all-gather.10.cloned.1.call-update) | async-done | bytes 16777232 | tf_op jit(solution)/shard_map/all_gather | solution.py:13
  381.6 65.4 %while.23 = (s32[]{:T(128)}, f32[4,128,128]{2,1,0:T(8,128)S(1)}, s32[]{:T(128)}, f32[64,4,128,128]{3,2,1,0:T(8,128)}, s32[]{:T(128)}, /*index=5*/s32[]{:T(128)}, s32[]{:T(128)}, s32[]{:T(128)}) while((s32[]{:T(128)}, f32[4,128,128]{2,1,0:T(8,128)S(1)}, s32[]{:T(128)}, f32[64,4,128,128]{3,2,1,0:T(8,128)}, s32[]{:T(128)}, /*index=5*/s32[]{:T(128)}, ...), condition=%wide.region_3.4_spmd, body=%wide.region_2.3_spmd.sunk | while | flops 65542 | bytes 786567 | solution.py:20
  381.6 1.0 bitcast_add_fusion.5
  382.7 1.0 bitcast_add_fusion.5
  383.7 1.0 bitcast_add_fusion.5
  384.7 1.0 bitcast_add_fusion.5
  385.8 1.0 bitcast_add_fusion.5
  386.8 1.0 bitcast_add_fusion.5
  388.9 1.0 bitcast_add_fusion.5
  393.0 1.0 bitcast_add_fusion.5
  397.2 1.0 bitcast_add_fusion.5
  398.2 1.0 bitcast_add_fusion.5
  400.3 1.0 bitcast_add_fusion.5
  401.3 1.0 bitcast_add_fusion.5
  403.4 1.0 bitcast_add_fusion.5
  404.5 1.0 bitcast_add_fusion.5
  406.5 1.0 bitcast_add_fusion.5
  407.6 1.0 bitcast_add_fusion.5
  408.6 1.0 bitcast_add_fusion.5
  409.7 1.0 bitcast_add_fusion.5
  411.7 1.0 bitcast_add_fusion.5
  412.8 1.0 bitcast_add_fusion.5
  414.8 1.0 bitcast_add_fusion.5
  415.9 1.0 bitcast_add_fusion.5
  418.0 1.0 bitcast_add_fusion.5
  419.0 1.0 bitcast_add_fusion.5
  421.1 1.0 bitcast_add_fusion.5
  422.1 1.0 bitcast_add_fusion.5
  423.2 1.0 bitcast_add_fusion.5
  424.2 1.0 bitcast_add_fusion.5
  425.2 1.0 bitcast_add_fusion.5
  426.3 1.0 bitcast_add_fusion.5
  428.4 1.0 bitcast_add_fusion.5
  429.4 1.0 bitcast_add_fusion.5
  431.5 1.0 bitcast_add_fusion.5
  432.5 1.0 bitcast_add_fusion.5
  434.6 1.0 bitcast_add_fusion.5
  435.6 1.0 bitcast_add_fusion.5
  436.7 1.0 bitcast_add_fusion.5
  437.7 1.0 bitcast_add_fusion.5
  438.7 1.0 bitcast_add_fusion.5
  439.8 1.0 bitcast_add_fusion.5
  440.8 1.0 bitcast_add_fusion.5
  441.9 1.0 bitcast_add_fusion.5
  442.9 1.0 bitcast_add_fusion.5
  445.0 1.0 bitcast_add_fusion.5
  446.0 1.0 bitcast_add_fusion.5
  449.2 181.5 %reduce-scatter.2.cloned.1.call-done = f32[512,32]{0,1:T(8,128)} async-done(((f32[512,2048]{0,1:T(8,128)}), f32[512,32]{0,1:T(8,128)}) %reduce-scatter.2.cloned.1.call-update) | async-done | bytes 65552 | tf_op jit(solution)/shard_map/reduce_scatter | solution.py:87
  630.8 1.5 broadcast_multiply_fusion
  (75 shorter events, 27.8 us)
Async XLA Ops:
  7.2 94.7 %copy-start = (bf16[256,512]{1,0:T(8,128)(2,1)S(1)}, bf16[256,512]{1,0:T(8,128)(2,1)}, u32[]{:S(2)}) copy-start(bf16[256,512]{1,0:T(8,128)(2,1)} %param.9) | copy-start | bytes 786436
  7.2 36.0 %copy-start.3 = (bf16[256,256]{1,0:T(8,128)(2,1)S(1)}, bf16[256,256]{1,0:T(8,128)(2,1)}, u32[]{:S(2)}) copy-start(bf16[256,256]{1,0:T(8,128)(2,1)} %param.12) | copy-start | bytes 393220
  7.2 92.2 %all-gather.6.cloned.1.call-start = ((), (), s32[]{:S(2)}) async-start(), calls=%async_computation.1 | async-start | bytes 2129920 | tf_op jit(solution)/shard_map/all_gather | solution.py:46
  7.9 231.9 %all-gather.8.cloned.1.call-start = ((), (), s32[]{:S(2)}) async-start(), calls=%async_computation.3 | async-start | bytes 17039360 | tf_op jit(solution)/shard_map/all_gather | solution.py:13
  11.0 370.6 %all-gather.10.cloned.1.call-start = ((), (), s32[]{:S(2)}) async-start(), calls=%async_computation.4 | async-start | bytes 17039360 | tf_op jit(solution)/shard_map/all_gather | solution.py:13
  11.1 4.6 collective-permute-start
  15.7 4.4 collective-permute-start.1
  20.1 4.4 collective-permute-start.2
  24.5 4.4 collective-permute-start.3
  28.9 4.4 collective-permute-start.4
  33.3 4.4 collective-permute-start.5
  37.7 4.5 collective-permute-start.6
  44.3 55.2 %copy-start.2 = (bf16[256,4096]{1,0:T(8,128)(2,1)}, bf16[256,4096]{1,0:T(8,128)(2,1)S(1)}, u32[]{:S(2)}) copy-start(bf16[256,4096]{1,0:T(8,128)(2,1)S(1)} %constant_dynamic-update-slice_fusion) | copy-start | bytes 6291460
  44.3 58.8 %copy-start.1 = (bf16[256,512]{1,0:T(8,128)(2,1)S(1)}, bf16[256,512]{1,0:T(8,128)(2,1)}, u32[]{:S(2)}) copy-start(bf16[256,512]{1,0:T(8,128)(2,1)} %param.10) | copy-start | bytes 786436
  103.0 527.8 %reduce-scatter.2.cloned.1.call-start = ((), (), s32[]{:S(2)}) async-start(), calls=%async_computation.2 | async-start | bytes 4259840 | tf_op jit(solution)/shard_map/reduce_scatter | solution.py:87
Sparse Core Ops, SparseCore 0:
  11.0 88.3 all-gather.5
  103.0 136.7 all-gather.7
  243.4 138.1 all-gather.9
  385.5 245.2 reduce-scatter.1
